TPU v7x, 32 devices: a whole 2x2x4 slice. The times are simulated.
32 devices in a mesh: img: 8 (over z, y), seq: 4 (over x, core).
Axes of the slice: x: 2, y: 2, z: 4, core: 2. Of those that a mesh axis runs over, the one named last changes fastest.
Arguments:
- tokens: float32 [8, 4096, 384], P('img', 'seq'), may hold values from -6 to 6
- valid_mask: int32 [8, 4096], P('img', 'seq'), may hold values from 0 to 1, as said below
- timesteps: int32 [8], P('img'), may hold values from 0 to 999
- class_ids: int32 [8], P('img'), may hold values from 0 to 999
- time_first: float32 [256, 384], replicated, may hold values from -0.375 to 0.375
- time_second: float32 [384, 384], replicated, may hold values from -0.3125 to 0.3125
- class_table: float32 [1000, 384], replicated, may hold values from -6 to 6
- ada_weight: float32 [384, 2304], replicated, may hold values from -0.3125 to 0.3125
- ada_bias: float32 [2304], replicated, may hold values from -3 to 3
- conv_taps: float32 [9, 384], replicated, may hold values from -2 to 2
- query_proj: float32 [384, 384], replicated, may hold values from -0.3125 to 0.3125
- key_proj: float32 [384, 384], replicated, may hold values from -0.3125 to 0.3125
- value_proj: float32 [384, 384], replicated, may hold values from -0.3125 to 0.3125
- decay_down: float32 [384, 16], replicated, may hold values from -0.3125 to 0.3125
- decay_up: float32 [16, 384], replicated, may hold values from -1.5 to 1.5
- decay_bias: float32 [384], replicated, may hold values from 0.5 to 6
- gate_proj: float32 [384, 384], replicated, may hold values from -0.3125 to 0.3125
- out_proj: float32 [384, 384], replicated, may hold values from -0.625 to 0.625
- mlp_up: float32 [384, 1536], replicated, may hold values from -0.3125 to 0.3125
- mlp_down: float32 [1536, 384], replicated, may hold values from -0.3125 to 0.3125
- cotangent: float32 [8, 4096, 384], P('img', 'seq'), may hold values from -6 to 6
Outputs:
- block_out: float32 [8, 4096, 384], P('img', 'seq')
- tokens_grad: float32 [8, 4096, 384], P('img', 'seq')
- time_first_grad: float32 [256, 384], replicated
- time_second_grad: float32 [384, 384], replicated
- class_table_grad: float32 [1000, 384], replicated
- ada_weight_grad: float32 [384, 2304], replicated
- ada_bias_grad: float32 [2304], replicated
- conv_taps_grad: float32 [9, 384], replicated
- query_proj_grad: float32 [384, 384], replicated
- key_proj_grad: float32 [384, 384], replicated
- value_proj_grad: float32 [384, 384], replicated
- decay_down_grad: float32 [384, 16], replicated
- decay_up_grad: float32 [16, 384], replicated
- decay_bias_grad: float32 [384], replicated
- gate_proj_grad: float32 [384, 384], replicated
- out_proj_grad: float32 [384, 384], replicated
- mlp_up_grad: float32 [384, 1536], replicated
- mlp_down_grad: float32 [1536, 384], replicated
Inputs may be any that keep to these rules, and one draw needn't show every extreme that they name: `valid_mask`: in each image the real patches are the first L of its 4096 patches, with 1024 <= L < 4096.
All inputs are finite; a program needn't handle non-finite values.
Results may differ from a plain program's by a relative error of at most 0.0003.
Values sent between devices are 32-bit elements; how exact they have to be, the bound alone decides.
No kernel may reach another device: no remote copies, remote signals or barrier semaphores. Data moves between devices by JAX's collectives and lax.ppermute only.
A program may use at most 320 MiB of HBM per device.

v0:
```python
import math
import jax
import jax.numpy as jnp
from jax import lax
from jax.sharding import PartitionSpec as P

HEADS = 6
HEAD_DIM = 64
CLASSES = 1000
FREQ = 256
GRID = 64
STRETCH = 64
HIGH = lax.Precision.HIGHEST


def extended(shard, sides, width):
    for axis, dim in sides:
        size, length = (lax.axis_size(axis), shard.shape[dim])
        up = [(i, (i + 1) % size) for i in range(size - 1)]
        down = [(j, i) for i, j in up]
        last = lax.slice_in_dim(shard, length - width, length, axis=dim)
        leading = lax.slice_in_dim(shard, 0, width, axis=dim)
        before = lax.ppermute(last, axis, up)
        after = lax.ppermute(leading, axis, down)
        shard = jnp.concatenate([before, shard, after], axis=dim)
    return shard


def carried_in(value, axis, join, neutral, backward):
    count, mine = (lax.axis_size(axis), lax.axis_index(axis))
    pieces = jax.tree.map(lambda part: lax.all_gather(part, axis), value)
    if backward:
        pieces = jax.tree.map(lambda part: part[::-1], pieces)
        mine = count - 1 - mine
    total = jax.tree.map(
        lambda part, zero: jnp.full_like(part, 0) + jnp.asarray(zero, part.dtype), value, neutral
    )

    def lap(position, total):
        longer = join(total, jax.tree.map(lambda part: part[position], pieces))
        return jax.tree.map(lambda new, old: jnp.where(position < mine, new, old), longer, total)

    return lax.fori_loop(0, count - 1, lap, total)


def product(left, right):
    return jnp.dot(left, right, precision=HIGH, preferred_element_type=jnp.float32)


def time_features(timesteps):
    half = FREQ // 2
    freqs = jnp.exp(-math.log(10000.0) * jnp.arange(half, dtype=jnp.float32) / half)
    angles = timesteps.astype(jnp.float32)[:, None] * freqs[None, :]
    return jnp.concatenate([jnp.cos(angles), jnp.sin(angles)], axis=1)


def condition(timesteps, class_ids, time_first, time_second, class_table, ada_weight, ada_bias):
    embed = product(jax.nn.silu(product(time_features(timesteps), time_first)), time_second)
    onehot = (class_ids[:, None] == jnp.arange(CLASSES, dtype=jnp.int32)[None, :]).astype(
        jnp.float32
    )
    embed = embed + product(onehot, class_table)
    return product(jax.nn.silu(embed), ada_weight) + ada_bias


def layer_norm(values):
    center = values - jnp.mean(values, axis=-1, keepdims=True)
    return center * lax.rsqrt(jnp.mean(center * center, axis=-1, keepdims=True) + 1e-06)


def pair_mix(query, keys, values, cumul):
    diff = cumul[..., :, None, :, :] - cumul[..., None, :, :, :]
    size = cumul.shape[-3]
    causal = (jnp.arange(size)[:, None] >= jnp.arange(size)[None, :])[:, :, None, None]
    weight = jnp.where(causal, jnp.exp(jnp.where(causal, diff, 0.0)), 0.0)
    scores = jnp.sum(query[..., :, None, :, :] * keys[..., None, :, :, :] * weight, axis=-1)
    return jnp.einsum("...tsh,...she->...the", scores, values, precision=HIGH)


def chain_join(earlier, later):
    return (later[0] * earlier[0], later[0][..., None] * earlier[1] + later[1])


def front(tokens, modul):
    pieces = jnp.split(modul, 6, axis=1)
    return layer_norm(tokens) * (1.0 + pieces[1][:, None]) + pieces[0][:, None]


def mixer_front(
    padded, keep, conv_taps, query_proj, key_proj, value_proj, decay_down, decay_up, decay_bias
):
    count, span, width = padded.shape
    length = span - 2 * GRID
    lines = length // GRID
    grid = jnp.pad(padded.reshape(count, lines + 2, GRID, width), ((0, 0), (0, 0), (1, 1), (0, 0)))
    mixed = jnp.zeros((count, lines, GRID, width), jnp.float32)
    for row in range(3):
        for col in range(3):
            mixed = mixed + conv_taps[row * 3 + col] * grid[:, row : row + lines, col : col + GRID]
    hidden = jax.nn.silu(mixed.reshape(count, length, width))
    query = product(hidden, query_proj) * HEAD_DIM ** (-0.5)
    keys = product(hidden, key_proj) * keep
    values = product(hidden, value_proj) * keep
    gates = (
        jax.nn.log_sigmoid(product(product(hidden, decay_down), decay_up) + decay_bias)
        / 16.0
        * keep
    )
    blocks = length // STRETCH

    def shaped(array):
        return array.reshape(count, blocks, STRETCH, HEADS, HEAD_DIM)

    query, keys, values, gates = (shaped(query), shaped(keys), shaped(values), shaped(gates))
    cumul = jnp.cumsum(gates, axis=2)
    group = math.gcd(count, max(1, 512 // length))

    def grouped(array):
        return array.reshape((count // group, group) + array.shape[1:])

    inner = lax.map(
        jax.checkpoint(lambda items: pair_mix(*items)),
        (grouped(query), grouped(keys), grouped(values), grouped(cumul)),
    )
    inner = inner.reshape(query.shape)
    decayed_query = query * jnp.exp(cumul)
    final = cumul[:, :, -1]
    carried = jnp.einsum(
        "ncshd,ncshe->nchde", keys * jnp.exp(final[:, :, None] - cumul), values, precision=HIGH
    )
    fades = jnp.exp(final)

    def advance(carry, items):
        total_fade, total_state = carry
        fade, state = items
        return (
            (fade * total_fade, fade[..., None] * total_state + state),
            (total_fade, total_state),
        )

    start = (jnp.ones_like(fades[:, 0]), jnp.zeros_like(carried[:, 0]))
    (dev_fade, dev_state), (pre_fade, pre_state) = lax.scan(
        advance, start, (jnp.moveaxis(fades, 1, 0), jnp.moveaxis(carried, 1, 0))
    )
    return (inner, decayed_query, pre_state, pre_fade, dev_fade, dev_state)


def tail(
    inner,
    decayed_query,
    pre_state,
    pre_fade,
    state_in,
    tokens,
    normed,
    modul,
    gate_proj,
    out_proj,
    mlp_up,
    mlp_down,
):
    count, length, width = tokens.shape
    shift_a, scale_a, gate_a, shift_b, scale_b, gate_b = jnp.split(modul, 6, axis=1)
    enter = pre_state + pre_fade[..., None] * state_in[None]
    outer = jnp.einsum("ncthd,cnhde->ncthe", decayed_query, enter, precision=HIGH)
    attended = (inner + outer).reshape(count, length, HEADS, HEAD_DIM)
    attended = attended * lax.rsqrt(jnp.mean(attended * attended, axis=-1, keepdims=True) + 1e-05)
    branch = product(
        attended.reshape(count, length, width) * jax.nn.silu(product(normed, gate_proj)), out_proj
    )
    middle = tokens + gate_a[:, None] * branch
    second = layer_norm(middle) * (1.0 + scale_b[:, None]) + shift_b[:, None]
    return middle + gate_b[:, None] * product(jax.nn.gelu(product(second, mlp_up)), mlp_down)


def body(
    tokens,
    valid_mask,
    timesteps,
    class_ids,
    time_first,
    time_second,
    class_table,
    ada_weight,
    ada_bias,
    conv_taps,
    query_proj,
    key_proj,
    value_proj,
    decay_down,
    decay_up,
    decay_bias,
    gate_proj,
    out_proj,
    mlp_up,
    mlp_down,
    cotangent,
):
    length = tokens.shape[1]

    def embed(first, second, table, weight, bias):
        return condition(timesteps, class_ids, first, second, table, weight, bias)

    modul, pull_embed = jax.vjp(embed, time_first, time_second, class_table, ada_weight, ada_bias)
    normed, pull_front = jax.vjp(front, tokens, modul)
    padded = extended(normed, (("seq", 1),), GRID)
    keep = valid_mask.astype(jnp.float32)[..., None]

    def mixer(pad_in, taps, q_weight, k_weight, v_weight, down_weight, up_weight, bias_in):
        return mixer_front(
            pad_in, keep, taps, q_weight, k_weight, v_weight, down_weight, up_weight, bias_in
        )

    parts, pull_mixer = jax.vjp(
        mixer, padded, conv_taps, query_proj, key_proj, value_proj, decay_down, decay_up, decay_bias
    )
    inner, decayed_query, pre_state, pre_fade, dev_fade, dev_state = parts
    state_in = carried_in(
        (dev_fade, dev_state),
        "seq",
        chain_join,
        (jnp.ones_like(dev_fade), jnp.zeros_like(dev_state)),
        False,
    )[1]
    block_out, pull_tail = jax.vjp(
        tail,
        inner,
        decayed_query,
        pre_state,
        pre_fade,
        state_in,
        tokens,
        normed,
        modul,
        gate_proj,
        out_proj,
        mlp_up,
        mlp_down,
    )
    (
        d_inner,
        d_query,
        d_pre_state,
        d_pre_fade,
        d_state,
        dx_tail,
        dn_tail,
        dmod_tail,
        g_gate,
        g_out,
        g_up,
        g_down,
    ) = pull_tail(cotangent)
    d_outgoing = carried_in(
        (dev_fade, d_state),
        "seq",
        chain_join,
        (jnp.ones_like(dev_fade), jnp.zeros_like(d_state)),
        True,
    )[1]
    d_dev_fade = jnp.sum(d_outgoing * state_in, axis=-1)
    pulled = pull_mixer((d_inner, d_query, d_pre_state, d_pre_fade, d_dev_fade, d_outgoing))
    d_pad = pulled[0]
    rims = jnp.concatenate([d_pad[:, :GRID], d_pad[:, -GRID:]], axis=1)
    beside_all = extended(rims, (("seq", 1),), GRID)
    d_normed = d_pad[:, GRID:-GRID] + dn_tail
    d_normed = d_normed + jnp.pad(beside_all[:, :GRID], ((0, 0), (0, length - GRID), (0, 0)))
    d_normed = d_normed + jnp.pad(beside_all[:, -GRID:], ((0, 0), (length - GRID, 0), (0, 0)))
    dx_front, dmod_front = pull_front(d_normed)
    tokens_grad = dx_tail + dx_front
    embed_grads = pull_embed(dmod_tail + dmod_front)
    first_grads = tuple(embed_grads) + tuple(pulled[1:])
    summed = lax.psum(first_grads + (g_gate, g_out, g_up, g_down), ("img", "seq"))
    return (
        block_out,
        tokens_grad,
        summed[0],
        summed[1],
        summed[2],
        summed[3],
        summed[4],
        summed[5],
        summed[6],
        summed[7],
        summed[8],
        summed[9],
        summed[10],
        summed[11],
        summed[12],
        summed[13],
        summed[14],
        summed[15],
    )


def solution(mesh):
    placed = (
        P("img", "seq", None),
        P("img", "seq"),
        P("img"),
        P("img"),
        P(),
        P(),
        P(),
        P(),
        P(),
        P(),
        P(),
        P(),
        P(),
        P(),
        P(),
        P(),
        P(),
        P(),
        P(),
        P(),
        P("img", "seq", None),
    )
    return jax.shard_map(
        body,
        mesh=mesh,
        in_specs=placed,
        out_specs=(
            P("img", "seq", None),
            P("img", "seq", None),
            P(),
            P(),
            P(),
            P(),
            P(),
            P(),
            P(),
            P(),
            P(),
            P(),
            P(),
            P(),
            P(),
            P(),
            P(),
            P(),
        ),
        check_vma=False,
    )
```

profile of v0, /device:TPU:0, one launch (start us, length us, event | category | flops | bytes accessed | tf_op | source)
XLA Modules:
  0.0 1686.3 jit_solution(18301640404507162143)
XLA Ops:
  38.6 5.8 fusion.95
  54.4 8.6 divide_multiply_fusion
  65.3 4.2 convolution_multiply_fusion.1
  79.3 5.7 convolution_multiply_fusion
  94.9 4.5 copy.361
  103.0 4.3 copy.370
  111.4 5.7 convolution_multiply_fusion.2
  133.9 4.3 reshape.1383
  152.4 6.4 exponential_multiply_fusion.1
  158.7 7.7 fusion.55
  168.5 105.6 %while.81 = (s32[]{:T(128)}, f32[1,6,64]{2,1,0:T(8,128)S(1)}, f32[1,6,64,64]{3,2,1,0:T(8,128)}, f32[16,1,6,64]{3,2,1,0:T(8,128)}, f32[16,1,6,64,64]{4,3,2,1,0:T(...) while((s32[]{:T(128)}, f32[1,6,64]{2,1,0:T(8,128)S(1)}, ...), condition=%wide.region_5.6_spmd.clone, body=%wide.region_4.5_spmd.clone.sunk | while | flops 99459 | bytes 711314 | solution.py:142
  274.1 6.3 all-gather
  281.0 11.8 all-gather.1
  292.9 7.4 while.82
  305.6 8.5 fusion.38
  314.1 83.2 %multiply_reduce_fusion.2 = f32[16,64,64,6]{2,3,1,0:T(8,128)} fusion(f32[16,64,6,64]{3,1,2,0:T(8,128)} %copy.357, f32[16,64,6,64]{3,2,1,0:T(8,128)} %copy.356, f32[16,64,6,64]{3,1,2,0:T(8,128)} %copy.353, f32[16,64,6,64]{3,2,1,0:T(8,128)} %copy.351, pred[64,64]{1,0:T(8,128)(4,1)S(1)} %copy-done.111), kind=kLoop, calls=%fused_computation.36 | loop fusion | flops 150601728 | bytes 7868416 | tf_op jit(solution)/shard_map/jvp()/while/body/eval_jaxpr/reduce_sum | solution.py:76
  397.2 8.8 multiply_reduce_fusion.6
  414.6 4.9 copy.445
  419.5 4.6 reshape.1384
  427.1 4.2 fusion.170
  432.0 10.6 fusion.91
  442.7 13.2 fusion.77
  455.9 13.1 fusion.53
  468.9 13.9 fusion.19
  482.8 11.6 fusion.173
  494.4 9.5 fusion.89
  514.8 4.2 fusion.79
  519.0 6.4 fusion.82
  525.4 6.9 fusion.134
  536.3 5.5 copy.382
  548.4 7.1 fusion.29
  555.4 7.6 multiply_reduce_fusion.3
  564.7 10.0 all-gather.2
  576.8 7.4 while.83
  588.1 154.1 %while.80 = (s32[]{:T(128)}, f32[1,6,64]{2,1,0:T(8,128)S(1)}, f32[1,6,64,64]{3,2,1,0:T(8,128)}, f32[16,1,6,64]{3,0,2,1:T(8,128)}, f32[16,1,6,64,64]{4,3,2,1,0:T(...) while((s32[]{:T(128)}, f32[1,6,64]{2,1,0:T(8,128)S(1)}, ...), condition=%wide.region_21.22_spmd, body=%wide.region_19.21_spmd.sunk | while | flops 99459 | bytes 1202857 | solution.py:142
  742.1 9.9 fusion.35
  752.0 7.8 fusion.33
  759.8 4.6 copy.392
  764.4 4.4 copy.401
  768.8 4.7 copy.410
  788.9 8.0 fusion.63
  796.9 4.2 copy.408
  801.1 253.6 %fusion.13 = (f32[16,64,6,64]{3,1,2,0:T(8,128)}, f32[16,64,6,64]{3,2,1,0:T(8,128)}, f32[16,64,6,64]{3,1,2,0:T(8,128)}, f32[16,64,64,6]{2,3,1,0:T(8,128)}, f32[16,64,6,64]{3,2,1,0:T(8,128)}) fusion(f32[16,64,6,64]{3,1,2,0:T(8,128)} %copy.410, f32[16,64,6,64]{3,2,1,0:T(8,128)S(1)} %copy-done.36, f32[16,64,64,6]{2,3,1,0:T(8,128)} %copy.408, ...), kind=kLoop, calls=%fused_computation.35 | loop fusion | flops 425852928 | bytes 15732736 | tf_op jit(solution)/shard_map/transpose(jvp())/while/body/eval_jaxpr/checkpoint/reduce_sum | solution.py:72
  1054.7 6.6 fusion.25
  1065.2 12.6 fusion.133
  1077.8 21.7 %broadcast_multiply_fusion.2 = (f32[1,16,64,6,64]{4,1,3,2,0:T(8,128)}, f32[1,16,64,6,64]{4,1,3,2,0:T(8,128)}, f32[1,16,64,6,64]{4,1,3,2,0:T(8,128)}, f32[1,16,64,6,64]{4,1,3,2,0:T(8,128)}, f32[1,16,64,6,64]{4,1,3,2,0:T(8,128)}) fusion(f32[16,64]{0,1:T(8,128)S(1)} %copy-done.69, f32[16,64,6,64]{3,1,2,0:T(8,128)} %get-tuple-element.880, ...), kind=kLoop, calls=%fused_computation.165 | loop fusion | flops 6291456 | bytes 23646208 | tf_op jit(solution)/shard_map/transpose(jvp())/mul | solution.py:102
  1099.6 5.1 fusion.43
  1108.5 4.5 reshape.1385
  1119.9 4.4 copy.427
  1128.4 7.9 fusion.175
  1136.3 6.0 fusion.176
  1146.7 4.6 reshape.1387
  1151.4 5.9 fusion.100
  1160.3 4.5 reshape.1386
  1164.7 4.9 fusion.102
  1169.8 6.4 multiply_reduce_fusion.15
  1187.1 4.4 copy.434
  1195.1 7.7 fusion.177
  1203.5 4.8 copy.435
  1212.0 7.7 fusion.178
  1242.4 7.1 fusion.167
  1266.6 4.1 add_add_fusion.3
  1273.7 116.7 %all-reduce.27.cloned.1.call-done = (f32[2304]{0:T(1024)}, f32[9,384]{1,0:T(8,128)}, f32[384,16]{0,1:T(8,128)}, f32[16,384]{1,0:T(8,128)}, f32[384]{0:T(512)}) async-done(((f32[2304]{0:T(1024)}, f32[9,384]{1,0:T(8,128)}, f32[384,16]{0,1:T(8,128)}, f32[16,384]{1,0:T(8,128)}, f32[384]{0:T(512)}), (f32[2304]{0:T(1024)}, f32[9,384]{1,0:T(8,128)}, f32[384,16]{0,1:T(8,128)}, f32[16,384]{1,0:T(8,128)}, ...) | async-done | bytes 73744 | tf_op jit(solution)/shard_map/psum | solution.py:273
  1390.4 269.6 %all-reduce.29.cloned.1.call-done = (f32[256,384]{1,0:T(8,128)}, f32[384,384]{1,0:T(8,128)}, f32[1000,384]{1,0:T(8,128)}, f32[384,2304]{1,0:T(8,128)}, f32[384,3...) async-done(((f32[256,384]{1,0:T(8,128)}, ...) | async-done | bytes 13725712 | tf_op jit(solution)/shard_map/psum | solution.py:273
  (677 shorter events, 545.6 us)
Async XLA Ops:
  7.2 14.7 copy-start
  16.5 8.5 copy-start.70
  25.1 7.2 copy-start.105
  27.3 21.4 %collective-permute-start.1 = (f32[1,64,384]{1,2,0:T(8,128)}, f32[1,64,384]{1,2,0:T(8,128)}, u32[]{:S(2)}, u32[]{:S(2)}) collective-permute-start(f32[1,64,384]{1,2,0:T(8,128)} %get-tuple-element.1026), channel_id=1, source_target_pairs={{1,0},{2,1},{3,2},{5,4},{6,5},{7,6},{9,8},{10,9},{11,10},{13,12},{... | collective-permute-start | bytes 294920 | tf_op jit(solution)/shard_map/ppermute | solution.py:24
  28.6 20.1 %collective-permute-start = (f32[1,64,384]{1,2,0:T(8,128)}, f32[1,64,384]{1,2,0:T(8,128)}, u32[]{:S(2)}, u32[]{:S(2)}) collective-permute-start(f32[1,64,384]{1,2,0:T(8,128)} %get-tuple-element.1027), channel_id=1, source_target_pairs={{0,1},{1,2},{2,3},{4,5},{5,6},{6,7},{8,9},{9,10},{10,11},{12,13},{... | collective-permute-start | bytes 294920 | tf_op jit(solution)/shard_map/ppermute | solution.py:23
  32.3 79.0 %copy-start.64 = (f32[1,1024]{1,0:T(1,128)}, f32[1,1024]{1,0:T(1,128)S(1)}, u32[]{:S(2)}) copy-start(f32[1,1024]{1,0:T(1,128)S(1)} %convert_element_type.14) | copy-start | bytes 12292
  37.2 17.2 %copy-start.95 = (f32[384]{0:T(512)}, f32[384]{0:T(512)S(1)}, u32[]{:S(2)}) copy-start(f32[384]{0:T(512)S(1)} %get-tuple-element.900) | copy-start | bytes 4612
  152.4 6.4 copy-start.7
  158.7 7.7 copy-start.19
  280.4 12.4 copy-start.68
  305.5 8.5 copy-start.111
  314.1 83.2 %copy-start.8 = (f32[16,64,6,64]{3,1,2,0:T(8,128)S(1)}, f32[16,64,6,64]{3,1,2,0:T(8,128)}, u32[]{:S(2)}) copy-start(f32[16,64,6,64]{3,1,2,0:T(8,128)} %copy.363) | copy-start | bytes 4718596
  426.4 5.0 copy-start.46
  431.3 63.1 %copy-start.9 = (f32[1,1024,384]{1,2,0:T(8,128)}, f32[1,1024,384]{1,2,0:T(8,128)S(1)}, u32[]{:S(2)}) copy-start(f32[1,1024,384]{1,2,0:T(8,128)S(1)} %get-tuple-element.1000) | copy-start | bytes 4718596
  432.0 10.6 copy-start.45
  432.0 10.6 copy-start.129
  442.6 13.2 copy-start.114
  519.0 6.4 copy-start.35
  519.0 6.4 copy-start.131
  541.7 4.7 copy-start.17
  548.3 7.1 copy-start.4
  548.4 7.1 copy-start.18
  742.1 9.9 copy-start.20
  742.1 9.9 copy-start.22
  801.1 253.6 %copy-start.5 = (f32[1,16,64,6,64]{2,4,3,1,0:T(8,128)S(1)}, f32[1,16,64,6,64]{2,4,3,1,0:T(8,128)}, u32[]{:S(2)}) copy-start(f32[1,16,64,6,64]{2,4,3,1,0:T(8,128)} %copy-done.4) | copy-start | bytes 4718596
  1065.2 12.6 copy-start.3
  1065.2 12.6 copy-start.66
  1065.2 12.6 copy-start.49
  1065.2 12.6 copy-start.69
  1128.3 7.9 copy-start.14
  1128.4 7.9 copy-start.26
  1136.3 6.0 copy-start.62
  1136.3 7.5 copy-start.28
  1151.4 6.0 copy-start.27
  1164.7 5.0 copy-start.16
  1164.7 5.0 copy-start.32
  1164.7 5.0 copy-start.63
  1164.7 5.0 copy-start.88
  1169.7 6.5 copy-start.96
  1169.7 6.5 copy-start.97
  1169.8 6.5 copy-start.98
  1169.8 6.5 copy-start.99
  1169.8 6.5 copy-start.100
  1169.8 6.5 copy-start.101
  1169.8 6.5 copy-start.102
  1169.8 6.5 copy-start.103
  1169.8 6.5 copy-start.104
  1211.9 7.8 copy-start.125
  1211.9 8.4 copy-start.124
  1211.9 9.0 copy-start.123
  1211.9 9.5 copy-start.122
  1212.0 10.1 copy-start.121
  1212.0 10.6 copy-start.120
  1224.8 12.3 copy-start.109
  1224.8 13.6 copy-start.110
  1224.8 17.6 %copy-start.71 = (f32[1024]{0:T(1024)S(1)}, f32[1024]{0:T(1024)}, u32[]{:S(2)}) copy-start(f32[1024]{0:T(1024)} %copy-done.70) | copy-start | bytes 12292
  1224.8 17.6 %copy-start.80 = (f32[384]{0:T(512)S(1)}, f32[384]{0:T(512)}, u32[]{:S(2)}) copy-start(f32[384]{0:T(512)} %copy-done.79) | copy-start | bytes 4612
  1231.3 11.1 collective-permute-start.3
  1232.6 9.8 collective-permute-start.2
  1242.4 7.1 copy-start.76
  1242.4 7.2 copy-start.13
  1242.4 7.2 copy-start.73
  1257.5 132.9 %all-reduce.27.cloned.1.call-start = ((), (), s32[]{:S(2)}) async-start(), calls=%async_computation | async-start | bytes 176128 | tf_op jit(solution)/shard_map/psum | solution.py:273
  1261.9 398.0 %all-reduce.29.cloned.1.call-start = ((), (), s32[]{:S(2)}) async-start(), calls=%async_computation.1 | async-start | bytes 27451392 | tf_op jit(solution)/shard_map/psum | solution.py:273
  (76 other events, 202.4 us)
Sparse Core Ops, SparseCore 0:
  1265.9 124.4 all-reduce.26
  1398.5 261.3 all-reduce.28
where the time goes:
time: 1700 us; the launch traced here: 1690 us
  other arithmetic  566 us (33%)
  local copies, waits for them, and re-layouts  415 us (24%)
  waiting for transfers between devices  386 us (23%)
  matrix products  264 us (16%)
  blocking collectives  28.2 us (2%)
  between operations  17.1 us (1%)
    psum x2, waiting for transfers between devices, body(): lax.psum(first_grads + (g_gate, g_out, g_up, g_down), ('img', 'seq'))  386 us
    reduce_sum x1, other arithmetic, pair_mix(): diff = cumul[..., :, None, :, :] - cumul[..., None, :, :, :]  254 us
    dot_general x33, matrix products, product(): jnp.dot(left, right, precision=HIGH, preferred_element_type=jnp.float32)  192 us
    reduce_sum x1, other arithmetic, pair_mix(): jnp.sum(query[..., :, None, :, :] * keys[..., None, :, :, :] * weight, ax...  83.2 us
    dynamic_update_slice x64, local copies, waits for them, and re-layouts, mixer_front(): lax.scan(advance, start, (jnp.moveaxis(fades, 1, 0), jnp.moveaxis(carried...  68 us
    unnamed x297, local copies, waits for them, and re-layouts  56.7 us
    dynamic_slice x32, local copies, waits for them, and re-layouts, mixer_front(): lax.scan(advance, start, (jnp.moveaxis(fades, 1, 0), jnp.moveaxis(carried...  53.4 us
    reshape x11, local copies, waits for them, and re-layouts, shaped(): return array.reshape(count, blocks, STRETCH, HEADS, HEAD_DIM)  43.4 us
  transfers between devices with their start and end apart: 6, of which 2 were waited for; matrix products, arithmetic and copies ran while one was open for 2% of the time, Pallas kernels for 0%

commit v1 on v0

--- a/solution.py
+++ b/solution.py
@@ -3,6 +3,7 @@
 import jax.numpy as jnp
 from jax import lax
 from jax.sharding import PartitionSpec as P
+from jax.lax import psum
 
 HEADS = 6
 HEAD_DIM = 64
@@ -270,7 +271,9 @@
     tokens_grad = dx_tail + dx_front
     embed_grads = pull_embed(dmod_tail + dmod_front)
     first_grads = tuple(embed_grads) + tuple(pulled[1:])
-    summed = lax.psum(first_grads + (g_gate, g_out, g_up, g_down), ("img", "seq"))
+    my_data = first_grads + (g_gate, g_out, g_up, g_down)
+    base_arr = psum(my_data, "seq")
+    summed = psum(base_arr, "img")
     return (
         block_out,
         tokens_grad,

time: 1700 us -> 2100 us (1.24)
  waiting for transfers between devices: 386 us -> 790 us
    psum x2 -> x4, waiting for transfers between devices: 386 us -> 790 us  [the longest x2 508 us: body(): summed = psum(base_arr, 'img')]
  transfers between devices with their start and end apart: 6 -> 8, of which waited for: 2 -> 4; matrix products, arithmetic and copies ran while one was open for 2% -> 2% of each run, Pallas kernels for 0% -> 0%
where the time goes in v1:
time: 2100 us; the launch traced here: 2090 us
  waiting for transfers between devices  790 us (38%)
  other arithmetic  566 us (27%)
  local copies, waits for them, and re-layouts  415 us (20%)
  matrix products  264 us (13%)
  blocking collectives  28.2 us (1%)
    psum x2, waiting for transfers between devices, body(): summed = psum(base_arr, 'img')  508 us
    psum x2, waiting for transfers between devices, body(): base_arr = psum(my_data, 'seq')  282 us
    reduce_sum x1, other arithmetic, pair_mix(): diff = cumul[..., :, None, :, :] - cumul[..., None, :, :, :]  254 us
    dot_general x33, matrix products, product(): jnp.dot(left, right, precision=HIGH, preferred_element_type=jnp.float32)  192 us
    reduce_sum x1, other arithmetic, pair_mix(): jnp.sum(query[..., :, None, :, :] * keys[..., None, :, :, :] * weight, ax...  83.2 us
    dynamic_update_slice x64, local copies, waits for them, and re-layouts, mixer_front(): lax.scan(advance, start, (jnp.moveaxis(fades, 1, 0), jnp.moveaxis(carried...  68 us
    unnamed x297, local copies, waits for them, and re-layouts  56.7 us
    dynamic_slice x32, local copies, waits for them, and re-layouts, mixer_front(): lax.scan(advance, start, (jnp.moveaxis(fades, 1, 0), jnp.moveaxis(carried...  53.4 us
  transfers between devices with their start and end apart: 8, of which 4 were waited for; matrix products, arithmetic and copies ran while one was open for 2% of the time, Pallas kernels for 0%

profile of v1, /device:TPU:0, one launch (start us, length us, event | category | flops | bytes accessed | tf_op | source)
XLA Modules:
  0.0 2089.5 jit_solution(7694720663115882120)
XLA Ops:
  38.6 5.8 fusion.95
  54.4 8.6 divide_multiply_fusion
  65.3 4.2 convolution_multiply_fusion.1
  79.4 5.7 convolution_multiply_fusion
  94.9 4.5 copy.361
  103.0 4.3 copy.370
  111.4 5.7 convolution_multiply_fusion.2
  134.0 4.3 reshape.1383
  152.4 6.4 exponential_multiply_fusion.1
  158.8 7.7 fusion.55
  168.6 105.6 %while.81 = (s32[]{:T(128)}, f32[1,6,64]{2,1,0:T(8,128)S(1)}, f32[1,6,64,64]{3,2,1,0:T(8,128)}, f32[16,1,6,64]{3,2,1,0:T(8,128)}, f32[16,1,6,64,64]{4,3,2,1,0:T(...) while((s32[]{:T(128)}, f32[1,6,64]{2,1,0:T(8,128)S(1)}, ...), condition=%wide.region_5.6_spmd.clone, body=%wide.region_4.5_spmd.clone.sunk | while | flops 99459 | bytes 711314 | solution.py:143
  274.1 6.3 all-gather
  281.1 11.8 all-gather.1
  292.9 7.4 while.82
  305.6 8.5 fusion.38
  314.1 83.2 %multiply_reduce_fusion.2 = f32[16,64,64,6]{2,3,1,0:T(8,128)} fusion(f32[16,64,6,64]{3,1,2,0:T(8,128)} %copy.357, f32[16,64,6,64]{3,2,1,0:T(8,128)} %copy.356, f32[16,64,6,64]{3,1,2,0:T(8,128)} %copy.353, f32[16,64,6,64]{3,2,1,0:T(8,128)} %copy.351, pred[64,64]{1,0:T(8,128)(4,1)S(1)} %copy-done.111), kind=kLoop, calls=%fused_computation.36 | loop fusion | flops 150601728 | bytes 7868416 | tf_op jit(solution)/shard_map/jvp()/while/body/eval_jaxpr/reduce_sum | solution.py:77
  397.3 8.8 multiply_reduce_fusion.6
  414.6 4.9 copy.445
  419.5 4.6 reshape.1384
  427.1 4.2 fusion.170
  432.1 10.6 fusion.91
  442.7 13.2 fusion.77
  455.9 13.1 fusion.53
  469.0 13.9 fusion.19
  482.8 11.6 fusion.173
  494.5 9.5 fusion.89
  514.8 4.2 fusion.79
  519.0 6.4 fusion.82
  525.4 6.9 fusion.134
  536.2 5.5 copy.382
  548.3 7.1 fusion.29
  555.4 7.6 multiply_reduce_fusion.3
  564.6 10.0 all-gather.2
  576.8 7.4 while.83
  588.0 154.0 %while.80 = (s32[]{:T(128)}, f32[1,6,64]{2,1,0:T(8,128)S(1)}, f32[1,6,64,64]{3,2,1,0:T(8,128)}, f32[16,1,6,64]{3,0,2,1:T(8,128)}, f32[16,1,6,64,64]{4,3,2,1,0:T(...) while((s32[]{:T(128)}, f32[1,6,64]{2,1,0:T(8,128)S(1)}, ...), condition=%wide.region_21.22_spmd, body=%wide.region_19.21_spmd.sunk | while | flops 99459 | bytes 1202857 | solution.py:143
  742.0 9.9 fusion.35
  751.8 7.8 fusion.33
  759.6 4.6 copy.392
  764.2 4.4 copy.401
  768.6 4.7 copy.410
  788.7 8.0 fusion.63
  800.9 253.6 %fusion.13 = (f32[16,64,6,64]{3,1,2,0:T(8,128)}, f32[16,64,6,64]{3,2,1,0:T(8,128)}, f32[16,64,6,64]{3,1,2,0:T(8,128)}, f32[16,64,64,6]{2,3,1,0:T(8,128)}, f32[16,64,6,64]{3,2,1,0:T(8,128)}) fusion(f32[16,64,6,64]{3,1,2,0:T(8,128)} %copy.410, f32[16,64,6,64]{3,2,1,0:T(8,128)S(1)} %copy-done.36, f32[16,64,64,6]{2,3,1,0:T(8,128)} %copy.408, ...), kind=kLoop, calls=%fused_computation.35 | loop fusion | flops 425852928 | bytes 15732736 | tf_op jit(solution)/shard_map/transpose(jvp())/while/body/eval_jaxpr/checkpoint/reduce_sum | solution.py:73
  1054.5 6.7 fusion.25
  1065.1 12.6 fusion.133
  1077.7 21.7 %broadcast_multiply_fusion.2 = (f32[1,16,64,6,64]{4,1,3,2,0:T(8,128)}, f32[1,16,64,6,64]{4,1,3,2,0:T(8,128)}, f32[1,16,64,6,64]{4,1,3,2,0:T(8,128)}, f32[1,16,64,6,64]{4,1,3,2,0:T(8,128)}, f32[1,16,64,6,64]{4,1,3,2,0:T(8,128)}) fusion(f32[16,64]{0,1:T(8,128)S(1)} %copy-done.69, f32[16,64,6,64]{3,1,2,0:T(8,128)} %get-tuple-element.880, ...), kind=kLoop, calls=%fused_computation.165 | loop fusion | flops 6291456 | bytes 23646208 | tf_op jit(solution)/shard_map/transpose(jvp())/mul | solution.py:103
  1099.4 5.1 fusion.43
  1108.3 4.5 reshape.1385
  1119.7 4.4 copy.427
  1128.2 7.9 fusion.175
  1136.1 6.0 fusion.176
  1146.6 4.6 reshape.1387
  1151.2 5.9 fusion.100
  1160.1 4.5 reshape.1386
  1164.6 4.9 fusion.102
  1169.7 6.4 multiply_reduce_fusion.15
  1186.9 4.4 copy.434
  1195.0 7.7 fusion.177
  1203.3 4.8 copy.435
  1211.8 7.7 fusion.178
  1242.2 7.1 fusion.167
  1262.7 32.1 %all-reduce.35.cloned.1.call-done = (f32[2304]{0:T(1024)}, f32[9,384]{1,0:T(8,128)}, f32[384,16]{0,1:T(8,128)}, f32[16,384]{1,0:T(8,128)}, f32[384]{0:T(512)}) async-done(((f32[2304]{0:T(1024)}, f32[9,384]{1,0:T(8,128)}, f32[384,16]{0,1:T(8,128)}, f32[16,384]{1,0:T(8,128)}, f32[384]{0:T(512)}), (f32[2304]{0:T(1024)}, f32[9,384]{1,0:T(8,128)}, f32[384,16]{0,1:T(8,128)}, f32[16,384]{1,0:T(8,128)}, ...) | async-done | bytes 73744 | tf_op jit(solution)/shard_map/psum | solution.py:275
  1294.9 249.9 %all-reduce.37.cloned.1.call-done = (f32[256,384]{1,0:T(8,128)}, f32[384,384]{1,0:T(8,128)}, f32[1000,384]{1,0:T(8,128)}, f32[384,2304]{1,0:T(8,128)}, f32[384,3...) async-done(((f32[256,384]{1,0:T(8,128)}, ...) | async-done | bytes 13725712 | tf_op jit(solution)/shard_map/psum | solution.py:275
  1555.6 63.8 %all-reduce.31.cloned.1.call-done = (f32[2304]{0:T(1024)}, f32[9,384]{1,0:T(8,128)}, f32[384,16]{0,1:T(8,128)}, f32[16,384]{1,0:T(8,128)}, f32[384]{0:T(512)}) async-done(((f32[2304]{0:T(1024)}, f32[9,384]{1,0:T(8,128)}, f32[384,16]{0,1:T(8,128)}, f32[16,384]{1,0:T(8,128)}, f32[384]{0:T(512)}), (f32[2304]{0:T(1024)}, f32[9,384]{1,0:T(8,128)}, f32[384,16]{0,1:T(8,128)}, f32[16,384]{1,0:T(8,128)}, ...) | async-done | bytes 73744 | tf_op jit(solution)/shard_map/psum | solution.py:276
  1619.4 444.0 %all-reduce.33.cloned.1.call-done = (f32[256,384]{1,0:T(8,128)}, f32[384,384]{1,0:T(8,128)}, f32[1000,384]{1,0:T(8,128)}, f32[384,2304]{1,0:T(8,128)}, f32[384,3...) async-done(((f32[256,384]{1,0:T(8,128)}, ...) | async-done | bytes 13725712 | tf_op jit(solution)/shard_map/psum | solution.py:276
  (683 shorter events, 553.7 us)
Async XLA Ops:
  7.2 14.7 copy-start
  16.5 8.5 copy-start.70
  25.1 7.2 copy-start.105
  27.3 21.4 %collective-permute-start.1 = (f32[1,64,384]{1,2,0:T(8,128)}, f32[1,64,384]{1,2,0:T(8,128)}, u32[]{:S(2)}, u32[]{:S(2)}) collective-permute-start(f32[1,64,384]{1,2,0:T(8,128)} %get-tuple-element.1042), channel_id=1, source_target_pairs={{1,0},{2,1},{3,2},{5,4},{6,5},{7,6},{9,8},{10,9},{11,10},{13,12},{... | collective-permute-start | bytes 294920 | tf_op jit(solution)/shard_map/ppermute | solution.py:25
  28.6 20.1 collective-permute-start
  32.3 79.1 %copy-start.64 = (f32[1,1024]{1,0:T(1,128)}, f32[1,1024]{1,0:T(1,128)S(1)}, u32[]{:S(2)}) copy-start(f32[1,1024]{1,0:T(1,128)S(1)} %convert_element_type.14) | copy-start | bytes 12292
  37.2 17.2 copy-start.95
  152.4 6.4 copy-start.7
  158.8 7.7 copy-start.19
  280.5 12.4 copy-start.68
  305.6 8.5 copy-start.111
  314.1 83.2 %copy-start.8 = (f32[16,64,6,64]{3,1,2,0:T(8,128)S(1)}, f32[16,64,6,64]{3,1,2,0:T(8,128)}, u32[]{:S(2)}) copy-start(f32[16,64,6,64]{3,1,2,0:T(8,128)} %copy.363) | copy-start | bytes 4718596
  431.4 63.1 %copy-start.9 = (f32[1,1024,384]{1,2,0:T(8,128)}, f32[1,1024,384]{1,2,0:T(8,128)S(1)}, u32[]{:S(2)}) copy-start(f32[1,1024,384]{1,2,0:T(8,128)S(1)} %get-tuple-element.1016) | copy-start | bytes 4718596
  432.0 10.6 copy-start.45
  432.1 10.6 copy-start.129
  442.7 13.2 copy-start.114
  518.9 6.4 copy-start.35
  519.0 6.4 copy-start.131
  548.3 7.1 copy-start.4
  548.3 7.1 copy-start.18
  742.0 9.9 copy-start.20
  742.0 9.9 copy-start.22
  800.9 253.6 %copy-start.5 = (f32[1,16,64,6,64]{2,4,3,1,0:T(8,128)S(1)}, f32[1,16,64,6,64]{2,4,3,1,0:T(8,128)}, u32[]{:S(2)}) copy-start(f32[1,16,64,6,64]{2,4,3,1,0:T(8,128)} %copy-done.4) | copy-start | bytes 4718596
  1065.0 12.6 copy-start.3
  1065.0 12.6 copy-start.66
  1065.0 12.6 copy-start.49
  1065.0 12.6 copy-start.69
  1128.2 7.9 copy-start.14
  1128.2 7.9 copy-start.26
  1136.1 6.0 copy-start.62
  1136.1 7.5 copy-start.28
  1151.2 6.0 copy-start.27
  1164.6 5.0 copy-start.16
  1164.6 5.0 copy-start.32
  1164.6 5.0 copy-start.63
  1164.6 5.0 copy-start.88
  1169.6 6.5 copy-start.96
  1169.6 6.5 copy-start.97
  1169.6 6.5 copy-start.98
  1169.6 6.5 copy-start.99
  1169.6 6.5 copy-start.100
  1169.6 6.5 copy-start.101
  1169.6 6.5 copy-start.102
  1169.6 6.5 copy-start.103
  1169.7 6.5 copy-start.104
  1211.7 7.8 copy-start.125
  1211.7 8.4 copy-start.124
  1211.7 8.9 copy-start.123
  1211.7 9.5 copy-start.122
  1211.7 10.0 copy-start.121
  1211.7 10.6 copy-start.120
  1224.6 12.3 copy-start.109
  1224.6 13.6 copy-start.110
  1224.6 17.6 copy-start.71
  1224.6 17.6 copy-start.80
  1231.1 11.1 collective-permute-start.3
  1232.4 9.8 collective-permute-start.2
  1242.1 7.1 copy-start.76
  1242.2 7.2 copy-start.13
  1242.2 7.2 copy-start.73
  1257.3 37.6 %all-reduce.35.cloned.1.call-start = ((), (), s32[]{:S(2)}) async-start(), calls=%async_computation.2 | async-start | bytes 176128 | tf_op jit(solution)/shard_map/psum | solution.py:275
  1261.7 283.1 %all-reduce.37.cloned.1.call-start = ((), (), s32[]{:S(2)}) async-start(), calls=%async_computation.3 | async-start | bytes 27451392 | tf_op jit(solution)/shard_map/psum | solution.py:275
  1262.7 356.7 %all-reduce.31.cloned.1.call-start = ((), (), s32[]{:S(2)}) async-start(), calls=%async_computation | async-start | bytes 176128 | tf_op jit(solution)/shard_map/psum | solution.py:276
  1294.9 768.6 %all-reduce.33.cloned.1.call-start = ((), (), s32[]{:S(2)}) async-start(), calls=%async_computation.1 | async-start | bytes 27451392 | tf_op jit(solution)/shard_map/psum | solution.py:276
  (78 other events, 212.2 us)
Sparse Core Ops, SparseCore 0:
  1261.9 32.8 all-reduce.34
  1300.7 243.9 all-reduce.36
  1548.7 70.6 all-reduce.30
  1625.7 437.6 all-reduce.32
